TPU v7x, 32 devices: a whole 2x2x4 slice. The times are simulated.
32 devices in a mesh: batch: 4 (over x, core), lat: 4 (over z), lon: 2 (over y).
Axes of the slice: x: 2, y: 2, z: 4, core: 2. Of those that a mesh axis runs over, the one named last changes fastest.
Arguments:
- tokens: bfloat16 [4, 2, 48, 48, 1024], P('batch', None, 'lat', 'lon'), may hold values from -6 to 6
- weights: bfloat16 [1024, 4096], P('batch')
- regions: int32 [2, 48, 48], P(None, 'lat', 'lon'), may hold values from 0 to 3
- offsets: int32 [2], replicated, may hold values from 1 to 11, as said below
Outputs:
- mixed: bfloat16 [4, 2, 48, 48, 1024], P('batch', None, 'lat', 'lon')
Inputs may be any that keep to these rules, and one draw needn't show every extreme that they name: `offsets`: element 0 lies from 1 to 5; element 1 equals 11.
All inputs are finite; a program needn't handle non-finite values.
Results may differ from a plain program's by a relative error of at most 0.0042.
Values may be sent and summed in bfloat16 or wider, within the bound.
A program may use at most 128 MiB of HBM per device.

v0:
```python
import jax
import jax.numpy as jnp
from jax import lax
from jax.sharding import PartitionSpec as P

HEADS = 16
WLEV = 2
WLAT = 6
WLON = 12


def from_behind(block, axis, distance):
    devices = range(lax.axis_size(axis))
    route = [((i - distance) % len(devices), i) for i in devices]
    return lax.ppermute(block, axis, route)


def layer_norm(field):
    field = field.astype(jnp.float32)
    average = jnp.mean(field, -1, keepdims=True)
    centred = field - average
    variance = jnp.mean(centred * centred, -1, keepdims=True)
    return (centred * lax.rsqrt(variance + 1e-05)).astype(jnp.bfloat16)


def windows(field):
    levels, rows_lat, cols_lon, features = field.shape
    field = field.reshape(
        levels // WLEV, WLEV, rows_lat // WLAT, WLAT, cols_lon // WLON, WLON, features
    )
    field = field.transpose(0, 2, 4, 1, 3, 5, 6)
    return field.reshape(-1, WLEV * WLAT * WLON, features)


def unwindows(field, levels, rows_lat, cols_lon):
    features = field.shape[-1]
    field = field.reshape(
        levels // WLEV, rows_lat // WLAT, cols_lon // WLON, WLEV, WLAT, WLON, features
    )
    field = field.transpose(0, 3, 1, 4, 2, 5, 6)
    return field.reshape(levels, rows_lat, cols_lon, features)


def attend(normed, all_weights, regions):
    levels, rows_lat, cols_lon, width = normed.shape
    qkv = jnp.dot(
        normed.reshape(-1, width), all_weights[:, : 3 * width], preferred_element_type=jnp.float32
    ).astype(jnp.bfloat16)
    qkv = windows(qkv.reshape(levels, rows_lat, cols_lon, 3 * width))
    num_windows, win_size = (qkv.shape[0], qkv.shape[1])
    head_size = width // HEADS
    queries = qkv[..., :width].reshape(num_windows, win_size, HEADS, head_size)
    keys_all = qkv[..., width : 2 * width].reshape(num_windows, win_size, HEADS, head_size)
    values_all = qkv[..., 2 * width :].reshape(num_windows, win_size, HEADS, head_size)
    scores = jnp.einsum(
        "wqhe,wkhe->whqk", queries, keys_all, preferred_element_type=jnp.float32
    ) * head_size ** (-0.5)
    region_ids = windows(regions[..., None])[..., 0]
    allowed = region_ids[:, None, :, None] == region_ids[:, None, None, :]
    scores = jnp.where(allowed, scores, -1e30)
    largest = jnp.max(scores, -1, keepdims=True)
    expsc = jnp.exp(scores - largest)
    attn_probs = (expsc / jnp.sum(expsc, -1, keepdims=True)).astype(jnp.bfloat16)
    mixed_out = jnp.einsum(
        "whqk,wkhe->wqhe", attn_probs, values_all, preferred_element_type=jnp.float32
    )
    mixed_out = mixed_out.astype(jnp.bfloat16).reshape(num_windows, win_size, width)
    return unwindows(mixed_out, levels, rows_lat, cols_lon)


def roll_forward(block_in, offsets):
    rows_lat, cols_lon = (block_in.shape[1], block_in.shape[2])
    from_next = from_behind(block_in[:, :WLAT], "lat", -1)
    joined = jnp.concatenate([block_in, from_next], axis=1)
    block_in = lax.dynamic_slice_in_dim(joined, offsets[0], rows_lat, 1)
    from_next = from_behind(block_in[:, :, :WLON], "lon", -1)
    joined = jnp.concatenate([block_in, from_next], axis=2)
    return lax.dynamic_slice_in_dim(joined, offsets[1], cols_lon, 2)


def roll_back(block_in, offsets):
    rows_lat, cols_lon = (block_in.shape[1], block_in.shape[2])
    from_prev = from_behind(block_in[:, rows_lat - WLAT :], "lat", 1)
    joined = jnp.concatenate([from_prev, block_in], axis=1)
    block_in = lax.dynamic_slice_in_dim(joined, WLAT - offsets[0], rows_lat, 1)
    from_prev = from_behind(block_in[:, :, cols_lon - WLON :], "lon", 1)
    joined = jnp.concatenate([from_prev, block_in], axis=2)
    return lax.dynamic_slice_in_dim(joined, WLON - offsets[1], cols_lon, 2)


def local(tokens, weights, regions, offsets):
    width = weights.shape[1] // 4
    all_weights = lax.all_gather(weights, "batch", axis=0, tiled=True)
    block_in = tokens[0]
    rolled = roll_forward(block_in, offsets)
    attended = attend(layer_norm(rolled), all_weights, regions)
    back_rolled = roll_back(attended, offsets)
    projected = jnp.dot(
        back_rolled.reshape(-1, width),
        all_weights[:, 3 * width :],
        preferred_element_type=jnp.float32,
    )
    mixed = block_in.astype(jnp.float32) + projected.reshape(block_in.shape)
    return mixed.astype(jnp.bfloat16)[None]


def solution(mesh):
    in_specs = (P("batch", None, "lat", "lon", None), P("batch", None), P(None, "lat", "lon"), P())
    out_specs = P("batch", None, "lat", "lon", None)
    return jax.shard_map(local, mesh=mesh, in_specs=in_specs, out_specs=out_specs, check_vma=False)
```

profile of v0, /device:TPU:0, one launch (start us, length us, event | category | flops | bytes accessed | tf_op | source)
XLA Modules:
  0.0 174.3 jit_solution(2364879644640626707)
XLA Ops:
  6.5 0.0 copy-start.2
  6.5 0.0 copy-start.7
  6.5 0.0 all-gather.2.cloned.1.call-start
  6.5 0.7 all-gather.2.cloned.1.call-update
  7.3 0.5 copy-done.2
  7.8 5.1 %collective-permute-start = (bf16[2,6,24,1024]{3,2,1,0:T(8,128)(2,1)S(1)}, bf16[2,6,24,1024]{3,2,1,0:T(8,128)(2,1)S(1)}, u32[]{:S(2)}, u32[]{:S(2)}) collective-permute-start(bf16[2,6,24,1024]{3,2,1,0:T(8,128)(2,1)S(1)} %slice.46), channel_id=1, source_target_pairs={{2,0},{4,2},{6,4},{0,6},{3,1},{5,3},{7,5},{1,7},{10,8},{12,10},{14... | collective-permute-start | bytes 1769480 | tf_op jit(solution)/shard_map/ppermute | solution.py:15
  12.9 0.0 copy-done.7
  13.0 0.6 fusion.30
  15.6 9.9 %collective-permute-done = bf16[2,6,24,1024]{3,2,1,0:T(8,128)(2,1)S(1)} collective-permute-done((bf16[2,6,24,1024]{3,2,1,0:T(8,128)(2,1)S(1)}, bf16[2,6,24,1024]{3,2,1,0:T(8,128)(2,1)S(1)}, u32[]{:S(2)}, u32[]{:S(2)}) %collective-permute-start) | collective-permute-done | bytes 589856 | tf_op jit(solution)/shard_map/ppermute | solution.py:15
  25.5 0.3 fusion.18
  25.9 0.0 copy-start.6
  25.9 0.1 slice.47
  26.0 0.6 copy.17
  26.6 1.6 collective-permute-start.1
  29.3 0.0 copy-done.6
  29.3 0.1 reshape_broadcast_in_dim.3
  29.4 0.1 eq.20
  30.1 0.8 broadcast_compare_fusion
  30.9 9.9 %collective-permute-done.1 = bf16[2,12,12,1024]{3,0,2,1:T(2,128)(2,1)S(1)} collective-permute-done((bf16[2,12,12,1024]{3,0,2,1:T(2,128)(2,1)S(1)}, bf16[2,12,12,1024]{3,0,2,1:T(2,128)(2,1)S(1)}, u32[]{:S(2)}, u32[]{:S(2)}) %collective-permute-start.1) | collective-permute-done | bytes 589856 | tf_op jit(solution)/shard_map/ppermute | solution.py:15
  40.8 0.1 copy.18
  41.0 1.1 convert_reduce_fusion
  42.1 0.4 fusion.13
  42.5 1.4 fusion.14
  43.9 26.1 %all-gather.2.cloned.1.call-done = bf16[1024,4096]{1,0:T(8,128)(2,1)} async-done(((bf16[256,4096]{1,0:T(8,128)(2,1)}), bf16[1024,4096]{1,0:T(8,128)(2,1)}) %all-gather.2.cloned.1.call-update) | async-done | bytes 8388624 | tf_op jit(solution)/shard_map/all_gather | solution.py:93
  69.9 7.0 %fusion.8 = bf16[576,3072]{1,0:T(8,128)(2,1)S(1)} fusion(bf16[576,1024]{1,0:T(8,128)(2,1)} %bitcast.51, bf16[1024,4096]{1,0:T(8,128)(2,1)} %all-gather.2.cloned.1.call-done), kind=kOutput, calls=%fused_computation.11 | convolution fusion | flops 3625648128 | bytes 11010048 | tf_op jit(solution)/shard_map/dot_general | solution.py:46
  76.9 3.5 %reshape_reshape.6 = bf16[1,2,2,6,2,12,3072]{6,5,4,3,2,1,0:T(8,128)(2,1)} reshape(bf16[576,3072]{1,0:T(8,128)(2,1)S(1)} %fusion.8) | data formatting | bytes 7077888 | tf_op jit(solution)/shard_map/reshape;reshape | solution.py:28
  80.5 7.8 %copy.19 = bf16[1,2,2,2,6,12,3072]{6,2,1,5,4,3,0:T(2,128)(2,1)} copy(bf16[1,2,2,2,6,12,3072]{6,5,2,4,1,3,0:T(8,128)(2,1)} %bitcast.43) | data formatting | bytes 7077888 | tf_op jit(solution)/shard_map/transpose | solution.py:31
  88.2 7.7 %reshape.45 = bf16[4,144,3072]{2,0,1:T(4,128)(2,1)S(1)} reshape(bf16[1,2,2,2,6,12,3072]{6,2,1,5,4,3,0:T(2,128)(2,1)} %copy.19) | data formatting | bytes 7077888 | tf_op jit(solution)/shard_map/reshape | solution.py:32
  95.9 2.7 %fusion.29 = (bf16[4,144,1024]{2,0,1:T(4,128)(2,1)}, bf16[4,144,1024]{2,0,1:T(4,128)(2,1)}, bf16[4,144,1024]{2,0,1:T(4,128)(2,1)}) fusion(bf16[4,144,3072]{2,0,1:T(4,128)(2,1)S(1)} %reshape.45), kind=kLoop, calls=%fused_computation.44 | loop fusion | bytes 7077888 | tf_op jit(solution)/shard_map/slice | solution.py:53
  98.6 0.0 copy-start.1
  98.6 4.1 %copy.22 = bf16[4,144,1024]{1,2,0:T(8,128)(2,1)} copy(bf16[4,144,1024]{2,0,1:T(4,128)(2,1)} %get-tuple-element.8) | data formatting | bytes 2359296 | tf_op jit(solution)/shard_map/slice | solution.py:52
  102.7 0.0 copy-start
  102.7 0.0 copy-done.1
  102.7 2.5 %copy.23 = bf16[4,144,1024]{1,2,0:T(8,128)(2,1)} copy(bf16[4,144,1024]{2,0,1:T(4,128)(2,1)S(1)} %copy-done.1) | data formatting | bytes 2359296 | tf_op jit(solution)/shard_map/slice | solution.py:53
  105.1 0.0 copy-start.4
  105.1 0.0 copy-start.5
  105.1 0.0 copy-done
  105.1 2.5 %copy.20 = bf16[4,144,1024]{1,2,0:T(8,128)(2,1)} copy(bf16[4,144,1024]{2,0,1:T(4,128)(2,1)S(1)} %copy-done) | data formatting | bytes 2359296 | tf_op jit(solution)/shard_map/slice | solution.py:54
  107.6 0.0 copy-done.4
  107.6 0.0 copy-done.5
  107.6 8.8 %fusion.31 = (f32[4,16,144]{2,1,0:T(8,128)S(1)}, f32[4,16,144,144]{2,3,1,0:T(8,128)}) fusion(pred[4,144,144]{1,2,0:T(8,128)(4,1)S(1)} %copy-done.5, bf16[4,144,16,64]{1,3,2,0:T(8,128)(2,1)S(1)} %bitcast.48, bf16[4,144,16,64]{1,3,2,0:T(8,128)(2,1)} %bitcast.49), kind=kOutput, calls=%fused_computation.46 | convolution fusion | flops 175177872 | bytes 7787520 | tf_op jit(solution)/shard_map/sub | solution.py:62
  116.4 6.5 %convert_bitcast_fusion = bf16[4,144,16,64]{1,3,2,0:T(8,128)(2,1)} fusion(bf16[4,144,16,64]{1,3,2,0:T(8,128)(2,1)} %bitcast.50, f32[4,16,144,144]{2,3,1,0:T(8,128)} %get-tuple-element.13, f32[4,16,144]{2,1,0:T(8,128)S(1)} %get-tuple-element.12), kind=kOutput, calls=%fused_computation.21 | convolution fusion | flops 173113344 | bytes 7704576 | tf_op jit(solution)/shard_map/whqk,wkhe->wqhe/dot_general | solution.py:64
  123.0 3.8 %copy.25 = bf16[4,144,16,64]{3,2,0,1:T(8,128)(2,1)S(1)} copy(bf16[4,144,16,64]{1,3,2,0:T(8,128)(2,1)} %convert_bitcast_fusion) | data formatting | bytes 2359296 | tf_op jit(solution)/shard_map/convert_element_type | solution.py:67
  126.8 1.4 reshape_reshape.7
  128.2 1.2 copy.26
  129.4 0.3 copy.27
  129.8 1.5 collective-permute-start.2
  132.7 14.4 %collective-permute-done.2 = bf16[2,6,24,1024]{3,2,1,0:T(8,128)(2,1)S(1)} collective-permute-done((bf16[2,6,24,1024]{3,2,1,0:T(8,128)(2,1)S(1)}, bf16[2,6,24,1024]{3,2,1,0:T(8,128)(2,1)S(1)}, u32[]{:S(2)}, u32[]{:S(2)}) %collective-permute-start.2) | collective-permute-done | bytes 589856 | tf_op jit(solution)/shard_map/ppermute | solution.py:15
  147.1 0.3 fusion.17
  147.4 0.0 copy-start.3
  147.4 0.2 slice.53
  147.6 0.6 copy.29
  148.2 1.5 collective-permute-start.3
  150.9 12.1 %collective-permute-done.3 = bf16[2,12,12,1024]{3,0,2,1:T(2,128)(2,1)S(1)} collective-permute-done((bf16[2,12,12,1024]{3,0,2,1:T(2,128)(2,1)S(1)}, bf16[2,12,12,1024]{3,0,2,1:T(2,128)(2,1)S(1)}, u32[]{:S(2)}, u32[]{:S(2)}) %collective-permute-start.3) | collective-permute-done | bytes 589856 | tf_op jit(solution)/shard_map/ppermute | solution.py:15
  163.0 0.1 copy.30
  163.2 0.0 copy-done.3
  163.2 4.3 %fusion.16 = bf16[1,2,12,24,1024]{4,3,2,1,0:T(8,128)(2,1)} fusion(bf16[1024,4096]{1,0:T(8,128)(2,1)} %all-gather.2.cloned.1.call-done, s32[]{:T(128)S(6)} %select_n.20, bf16[2,12,12,1024]{3,2,1,0:T(8,128)(2,1)S(1)} %copy.30, bf16[2,12,24,1024]{3,2,1,0:T(8,128)(2,1)S(1)} %fusion.17, bf16[1,2,12,24,1024]{4,3,2,1,0:T(8,128)(2,1)S(1)} %copy-done.3), kind=kOutput, calls=%fused_computation.30 | convolution fusion | flops 1212088320 | bytes 6225924 | tf_op jit(solution)/shard_map/dot_general | solution.py:98
  (5 shorter events, 0.1 us)
Async XLA Ops:
  6.5 1.3 copy-start.2
  6.5 6.4 %copy-start.7 = (s32[2]{0:T(128)S(1)}, s32[2]{0:T(128)}, u32[]{:S(2)}) copy-start(s32[2]{0:T(128)} %param.7) | copy-start | bytes 28
  6.5 63.4 %all-gather.2.cloned.1.call-start = ((), (), s32[]{:S(2)}) async-start(), calls=%async_computation | async-start | bytes 10485760 | tf_op jit(solution)/shard_map/all_gather | solution.py:93
  7.8 17.7 %collective-permute-start = (bf16[2,6,24,1024]{3,2,1,0:T(8,128)(2,1)S(1)}, bf16[2,6,24,1024]{3,2,1,0:T(8,128)(2,1)S(1)}, u32[]{:S(2)}, u32[]{:S(2)}) collective-permute-start(bf16[2,6,24,1024]{3,2,1,0:T(8,128)(2,1)S(1)} %slice.46), channel_id=1, source_target_pairs={{2,0},{4,2},{6,4},{0,6},{3,1},{5,3},{7,5},{1,7},{10,8},{12,10},{14... | collective-permute-start | bytes 1769480 | tf_op jit(solution)/shard_map/ppermute | solution.py:15
  25.9 3.4 %copy-start.6 = (s32[2,12,24]{2,0,1:T(2,128)S(1)}, s32[2,12,24]{2,0,1:T(2,128)}, u32[]{:S(2)}) copy-start(s32[2,12,24]{2,0,1:T(2,128)} %param.6) | copy-start | bytes 6916
  26.6 14.3 %collective-permute-start.1 = (bf16[2,12,12,1024]{3,0,2,1:T(2,128)(2,1)S(1)}, bf16[2,12,12,1024]{3,0,2,1:T(2,128)(2,1)S(1)}, u32[]{:S(2)}, u32[]{:S(2)}) collective-permute-start(bf16[2,12,12,1024]{3,0,2,1:T(2,128)(2,1)S(1)} %copy.17), channel_id=1, source_target_pairs={{1,0},{0,1},{3,2},{2,3},{5,4},{4,5},{7,6},{6,7},{9,8},{8,9},{11,10... | collective-permute-start | bytes 1769480 | tf_op jit(solution)/shard_map/ppermute | solution.py:15
  98.6 4.1 %copy-start.1 = (bf16[4,144,1024]{2,0,1:T(4,128)(2,1)S(1)}, bf16[4,144,1024]{2,0,1:T(4,128)(2,1)}, u32[]{:S(2)}) copy-start(bf16[4,144,1024]{2,0,1:T(4,128)(2,1)} %get-tuple-element.7) | copy-start | bytes 3538948
  102.7 2.5 %copy-start = (bf16[4,144,1024]{2,0,1:T(4,128)(2,1)S(1)}, bf16[4,144,1024]{2,0,1:T(4,128)(2,1)}, u32[]{:S(2)}) copy-start(bf16[4,144,1024]{2,0,1:T(4,128)(2,1)} %get-tuple-element.9) | copy-start | bytes 3538948
  105.1 2.5 %copy-start.4 = (bf16[4,144,1024]{1,2,0:T(8,128)(2,1)S(1)}, bf16[4,144,1024]{1,2,0:T(8,128)(2,1)}, u32[]{:S(2)}) copy-start(bf16[4,144,1024]{1,2,0:T(8,128)(2,1)} %copy.22) | copy-start | bytes 3538948
  105.1 2.5 %copy-start.5 = (pred[4,144,144]{1,2,0:T(8,128)(4,1)S(1)}, pred[4,144,144]{1,2,0:T(8,128)(4,1)}, u32[]{:S(2)}) copy-start(pred[4,144,144]{1,2,0:T(8,128)(4,1)} %broadcast_compare_fusion) | copy-start | bytes 248836
  129.8 17.3 %collective-permute-start.2 = (bf16[2,6,24,1024]{3,2,1,0:T(8,128)(2,1)S(1)}, bf16[2,6,24,1024]{3,2,1,0:T(8,128)(2,1)S(1)}, u32[]{:S(2)}, u32[]{:S(2)}) collective-permute-start(bf16[2,6,24,1024]{3,2,1,0:T(8,128)(2,1)S(1)} %slice.52), channel_id=1, source_target_pairs={{6,0},{0,2},{2,4},{4,6},{7,1},{1,3},{3,5},{5,7},{14,8},{8,10},{10,... | collective-permute-start | bytes 1769480 | tf_op jit(solution)/shard_map/ppermute | solution.py:15
  147.4 15.8 %copy-start.3 = (bf16[1,2,12,24,1024]{4,3,2,1,0:T(8,128)(2,1)S(1)}, bf16[1,2,12,24,1024]{4,3,2,1,0:T(8,128)(2,1)}, u32[]{:S(2)}) copy-start(bf16[1,2,12,24,1024]{4,3,2,1,0:T(8,128)(2,1)} %param.4) | copy-start | bytes 3538948
  148.2 14.8 %collective-permute-start.3 = (bf16[2,12,12,1024]{3,0,2,1:T(2,128)(2,1)S(1)}, bf16[2,12,12,1024]{3,0,2,1:T(2,128)(2,1)S(1)}, u32[]{:S(2)}, u32[]{:S(2)}) collective-permute-start(bf16[2,12,12,1024]{3,0,2,1:T(2,128)(2,1)S(1)} %copy.29), channel_id=1, source_target_pairs={{1,0},{0,1},{3,2},{2,3},{5,4},{4,5},{7,6},{6,7},{9,8},{8,9},{11,10... | collective-permute-start | bytes 1769480 | tf_op jit(solution)/shard_map/ppermute | solution.py:15
Sparse Core Ops, SparseCore 0:
  8.9 60.9 all-gather.1
where the time goes:
time: 175 us; the launch traced here: 174 us
  waiting for transfers between devices  73.1 us (42%)
  local copies, waits for them, and re-layouts  40.6 us (23%)
  matrix products  26.7 us (15%)
  between operations  19.9 us (11%)
  starting transfers between devices  9.77 us (6%)
  other arithmetic  4.29 us (2%)
    ppermute x4, waiting for transfers between devices, from_behind(): return lax.ppermute(block, axis, route)  46.3 us
    all_gather x1, waiting for transfers between devices, local(): all_weights = lax.all_gather(weights, 'batch', axis=0, tiled=True)  26.1 us
    ppermute x4, starting transfers between devices, from_behind(): return lax.ppermute(block, axis, route)  9.77 us
    sub x1, matrix products, attend(): expsc = jnp.exp(scores - largest)  8.82 us
    transpose x1, local copies, waits for them, and re-layouts, windows(): field = field.transpose(0, 2, 4, 1, 3, 5, 6)  7.79 us
    reshape x1, local copies, waits for them, and re-layouts, windows(): return field.reshape(-1, WLEV * WLAT * WLON, features)  7.66 us
    dot_general x1, matrix products, attend(): jnp.dot(normed.reshape(-1, width), all_weights[:, :3 * width], preferred_...  6.98 us
    dot_general x1, matrix products, attend(): jnp.einsum('whqk,wkhe->wqhe', attn_probs, values_all, preferred_element_t...  6.52 us
  transfers between devices with their start and end apart: 5, of which 5 were waited for; matrix products, arithmetic and copies ran while one was open for 3% of the time, Pallas kernels for 0%

commit v1 on v0

v1 whole, which is shorter than its diff:
```python
import functools

import jax
import jax.numpy as jnp
from jax import lax
from jax.experimental import pallas as pl
from jax.experimental.pallas import tpu as pltpu
from jax.sharding import PartitionSpec as P

HEADS = 16
WLEV = 2
WLAT = 6
WLON = 12
GROUPS = 4
HALO = WLAT - 1
MESH = pl.DeviceIdType.MESH


def normalise(x):
    average = jnp.mean(x, -1, keepdims=True)
    centred = x - average
    variance = jnp.mean(centred * centred, -1, keepdims=True)
    return centred * lax.rsqrt(variance + 1e-05)


def kernel(
    sizes,
    off_ref, tok_ref, w_ref, edge_ref, mask_ref, out_ref,
    wqkv, wout, ext, edge_ext, mask, xw, xn, qkv, ow, nat, ret, ymat,
    local_sem, w_send, w_recv, h_send, h_recv, r_send, r_recv, *parts,
):
    attn, ret_ext = parts[:GROUPS], parts[GROUPS:]
    nb, nlat, nlon = sizes
    levels, rows, cols, width = tok_ref.shape
    win = WLEV * WLAT * WLON
    gw = width // GROUPS
    depth = w_ref.shape[0]
    half = depth // 2
    chips = nb // 2
    b, lat, lon = lax.axis_index("batch"), lax.axis_index("lat"), lax.axis_index("lon")
    chip, core = b // 2, b % 2
    side = lon % 2

    def at(db=None, dlat=0, dlon=0):
        return (
            b if db is None else db,
            (lat + dlat + nlat) % nlat,
            (lon + dlon + nlon) % nlon,
        )

    partner = (chip * 2 + 1 - core, lat, lon)
    across = (b, lat, lon + 1 - 2 * side)
    far = [(((chip + k) % chips) * 2 + core, lat, lon) for k in range(1, chips)]
    greeted = [partner, across] + far + [
        at(dlat=-1), at(dlat=1), at(dlon=1), at(dlon=-1),
        at(dlat=-1, dlon=1), at(dlat=1, dlon=-1),
    ]

    def chunk(g):
        return wqkv.at[g] if g < GROUPS else wout

    def own_loads(g):
        rows_here = pl.ds(pl.multiple_of(b * depth, depth), depth)
        if g == GROUPS:
            return [pltpu.make_async_copy(
                w_ref.at[:, pl.ds(3 * width, width)], wout.at[rows_here], local_sem.at[3 * g])]
        return [
            pltpu.make_async_copy(
                w_ref.at[:, pl.ds(t * width + g * gw, gw)],
                wqkv.at[g, rows_here, pl.ds(t * gw, gw)],
                local_sem.at[3 * g + t],
            )
            for t in range(3)
        ]

    loads = [own_loads(g) for g in range(GROUPS + 1)]
    for group in loads:
        for c in group:
            c.start()
    tok_load = pltpu.make_async_copy(tok_ref, ext.at[:, 0:rows], local_sem.at[3 * GROUPS + 1])
    edge_load_sem = local_sem.at[3 * GROUPS + 2]
    tok_load.start()
    mask_load = pltpu.make_async_copy(mask_ref.at[0], mask.at[1], edge_load_sem)
    mask_load.start()

    barrier = pltpu.get_barrier_semaphore()
    for device in greeted:
        pl.semaphore_signal(barrier, inc=1, device_id=device, device_id_type=MESH)
    pl.semaphore_wait(barrier, len(greeted))

    def send(src, dst, ssem, rsem, device):
        c = pltpu.make_async_remote_copy(
            src_ref=src, dst_ref=dst, send_sem=ssem, recv_sem=rsem,
            device_id=device, device_id_type=MESH,
        )
        c.start()
        return c

    def piece(g, owner, part):
        return chunk(g).at[pl.ds(pl.multiple_of(owner * depth + part * half, half), half)]

    nsem = 1 + 4 * (chips - 1)
    sent = []

    def send_w(g, slot, ref, device):
        i = g * nsem + slot
        c = send(ref, ref, w_send.at[i], w_recv.at[i], device)
        sent.append(c)
        return c

    xs = {}
    halos = []
    core_copies = {g: [] for g in range(GROUPS + 1)}
    ys = {}

    def first(g):
        for c in loads[g]:
            c.wait()
        for k in range(1, chips):
            xs[g, k] = send_w(g, 4 * k - 3, piece(g, b, side), far[k - 1])
        mine = chunk(g).at[pl.ds(pl.multiple_of(b * depth, depth), depth)]
        core_copies[g].append(send_w(g, 0, mine, partner))

    def origin(k):
        return ((chip + chips - k) % chips) * 2 + core

    def relay(g):
        for k in range(1, chips):
            xs[g, k].wait_recv()
            got = piece(g, origin(k), side)
            ys[g, k] = send_w(g, 4 * k - 2, got, across)
            core_copies[g].append(send_w(g, 4 * k - 1, got, partner))

    def finish(g):
        for k in range(1, chips):
            ys[g, k].wait_recv()
            core_copies[g].append(send_w(g, 4 * k, piece(g, origin(k), 1 - side), partner))
        for c in core_copies[g]:
            c.wait_recv()

    first(0)
    halos.append(send(edge_ref, edge_ext.at[:, 0:rows], h_send.at[0], h_recv.at[0], at(dlon=1)))
    halos.append(send(edge_ref, edge_ext.at[:, rows:2 * rows], h_send.at[1], h_recv.at[1], at(dlat=-1, dlon=1)))
    halos.append(send(tok_ref.at[:, 0:HALO], ext.at[:, rows:rows + HALO], h_send.at[2], h_recv.at[2], at(dlat=-1)))
    halos.append(send(mask_ref.at[1], mask.at[0], h_send.at[3], h_recv.at[3], at(dlon=1)))
    for g in range(1, GROUPS + 1):
        first(g)

    shift = off_ref[0]
    relay(0)
    tok_load.wait()
    mask_load.wait()
    for c in halos:
        c.wait_recv()
    for l in range(levels):
        for i in range(rows):
            x = normalise(ext[l, i + shift].astype(jnp.float32))
            e = normalise(edge_ext[l, i + shift])
            base = (i // WLAT) * 2 * win + l * WLAT * WLON + (i % WLAT) * WLON
            xw[base:base + 1, :] = e
            xw[base + 1:base + WLON, :] = x[0:WLON - 1]
            xw[base + win:base + win + WLON, :] = x[WLON - 1:2 * WLON - 1]
    nwin = (rows // WLAT) * (cols // WLON)
    for w in range(nwin):
        xn[w * win:(w + 1) * win, :] = xw[w * win:(w + 1) * win, :].astype(jnp.bfloat16)

    lane = lax.broadcasted_iota(jnp.int32, (win, 128), 1)
    ones = jnp.ones((win, 128), jnp.bfloat16)
    hs = width // HEADS

    def attention(g):
        for t in range(3):
            part = jnp.dot(
                xn[...], wqkv[g, :, t * gw:(t + 1) * gw], preferred_element_type=jnp.float32
            ).astype(jnp.bfloat16)
            for w in range(nwin):
                qkv[w, :, t * gw:(t + 1) * gw] = part[w * win:(w + 1) * win]

        def window(w, carry):
            allowed = mask[w % 2, w // 2].astype(jnp.float32) > 0.5
            for pair in range(gw // 128):
                q = qkv[w, :, pair * 128:(pair + 1) * 128]
                k = qkv[w, :, gw + pair * 128:gw + (pair + 1) * 128]
                v = qkv[w, :, 2 * gw + pair * 128:2 * gw + (pair + 1) * 128]
                vones = jnp.concatenate([v, ones], axis=1)
                outs = []
                for h in range(128 // hs):
                    keep = (lane // hs == h).astype(jnp.float32) * (hs ** -0.5)
                    qh = (q.astype(jnp.float32) * keep).astype(jnp.bfloat16)
                    s = lax.dot_general(
                        qh, k, (((1,), (1,)), ((), ())), preferred_element_type=jnp.float32
                    )
                    s = jnp.where(allowed, s, -1e30)
                    e = jnp.exp(s - jnp.max(s, -1, keepdims=True)).astype(jnp.bfloat16)
                    o = jnp.dot(e, vones, preferred_element_type=jnp.float32)
                    outs.append(o[:, :128] / o[:, 128:])
                ow[w, :, pair * 128:(pair + 1) * 128] = jnp.where(lane < hs, outs[0], outs[1])
            return carry

        lax.fori_loop(0, nwin, window, 0)
        gs = slice(g * gw, (g + 1) * gw)
        for l in range(levels):
            for i in range(rows):
                r = l * WLAT * WLON + (i % WLAT) * WLON
                w = (i // WLAT) * 2
                ret[g, l, i] = ow[w, r:r + 1, :].astype(jnp.bfloat16).astype(jnp.float32)
                nat[l, i, 0:WLON - 1, :] = ow[w, r + 1:r + WLON, :]
                nat[l, i, WLON - 1:2 * WLON - 1, :] = ow[w + 1, r:r + WLON, :]
                attn[g][l, HALO + i] = nat[l, i].astype(jnp.bfloat16)
        back = [
            send(attn[g].at[:, rows:rows + HALO], attn[g].at[:, 0:HALO],
                 r_send.at[3 * g], r_recv.at[3 * g], at(dlat=1)),
            send(ret.at[g], ret_ext[g].at[:, rows:2 * rows],
                 r_send.at[3 * g + 1], r_recv.at[3 * g + 1], at(dlon=-1)),
            send(ret.at[g], ret_ext[g].at[:, 0:rows],
                 r_send.at[3 * g + 2], r_recv.at[3 * g + 2], at(dlat=1, dlon=-1)),
        ]
        return back

    nat[:, :, cols - 1:cols, :] = jnp.zeros((levels, rows, 1, gw), jnp.float32)
    row_id = lax.broadcasted_iota(jnp.int32, (cols, gw), 0)
    backs = []

    def gather(g):
        for c in backs[g]:
            c.wait_recv()
        for l in range(levels):
            for i in range(rows):
                a = attn[g][l, HALO + i - shift].astype(jnp.float32)
                e = ret_ext[g][l, rows + i - shift]
                r = (l * rows + i) * cols
                ymat[r:r + cols, g * gw:(g + 1) * gw] = jnp.where(row_id == cols - 1, e, a)

    for g in range(GROUPS):
        relay(g + 1)
        finish(g)
        backs.append(attention(g))
        if g > 0:
            gather(g - 1)
    finish(GROUPS)
    gather(GROUPS - 1)

    for l in range(levels):
        for j in range(rows // WLAT):
            r = (l * rows + j * WLAT) * cols
            y = ymat[r:r + WLAT * cols, :].astype(jnp.bfloat16)
            p = jnp.dot(y, wout[...], preferred_element_type=jnp.float32)
            here = slice(j * WLAT, (j + 1) * WLAT)
            t = ext[l, here].astype(jnp.float32)
            out_ref[l, here] = (t + p.reshape(t.shape)).astype(jnp.bfloat16)

    for c in sent + halos + sum(backs, []):
        c.wait_send()


def window_ids(regions):
    levels, rows, cols = regions.shape
    field = regions.reshape(levels, rows // WLAT, WLAT, cols // WLON, WLON)
    return field.transpose(3, 1, 0, 2, 4).reshape(cols // WLON, rows // WLAT, -1)


def local(sizes, tokens, weights, regions, offsets):
    block = tokens[0]
    levels, rows, cols, width = block.shape
    win = WLEV * WLAT * WLON
    nwin = (rows // WLAT) * (cols // WLON)
    gw = width // GROUPS
    edge = block[:, :, cols - 1:, :].astype(jnp.float32)
    ids = window_ids(regions)
    mask = (ids[..., :, None] == ids[..., None, :]).astype(jnp.bfloat16)
    nw = (GROUPS + 1) * (1 + 4 * (sizes[0] // 2 - 1))
    bf, f32 = jnp.bfloat16, jnp.float32
    dma = pltpu.SemaphoreType.DMA
    anywhere = pl.BlockSpec(memory_space=pl.ANY)
    out = pl.pallas_call(
        functools.partial(kernel, sizes),
        out_shape=jax.ShapeDtypeStruct(block.shape, bf),
        in_specs=[pl.BlockSpec(memory_space=pltpu.SMEM)] + [anywhere] * 4,
        out_specs=pl.BlockSpec(memory_space=pltpu.VMEM),
        scratch_shapes=[
            pltpu.VMEM((GROUPS, width, 3 * gw), bf),
            pltpu.VMEM((width, width), bf),
            pltpu.VMEM((levels, rows + HALO, cols, width), bf),
            pltpu.VMEM((levels, 2 * rows, 1, width), f32),
            pltpu.VMEM((2, rows // WLAT, win, win), bf),
            pltpu.VMEM((nwin * win, width), f32),
            pltpu.VMEM((nwin * win, width), bf),
            pltpu.VMEM((nwin, win, 3 * gw), bf),
            pltpu.VMEM((nwin, win, gw), f32),
            pltpu.VMEM((levels, rows, cols, gw), f32),
            pltpu.VMEM((GROUPS, levels, rows, 1, gw), f32),
            pltpu.VMEM((levels * rows * cols, width), f32),
            dma((3 * GROUPS + 3,)),
            dma((nw,)),
            dma((nw,)),
            dma((4,)),
            dma((4,)),
            dma((3 * GROUPS,)),
            dma((3 * GROUPS,)),
        ]
        + [pltpu.VMEM((levels, rows + HALO, cols, gw), bf)] * GROUPS
        + [pltpu.VMEM((levels, 2 * rows, 1, gw), f32)] * GROUPS,
        compiler_params=pltpu.CompilerParams(
            collective_id=0, has_side_effects=True, vmem_limit_bytes=56 * 1024 * 1024
        ),
    )(offsets, block, weights, edge, mask)
    return out[None]


def solution(mesh):
    sizes = (mesh.shape["batch"], mesh.shape["lat"], mesh.shape["lon"])
    in_specs = (P("batch", None, "lat", "lon", None), P("batch", None), P(None, "lat", "lon"), P())
    out_specs = P("batch", None, "lat", "lon", None)
    return jax.shard_map(
        functools.partial(local, sizes), mesh=mesh, in_specs=in_specs, out_specs=out_specs, check_vma=False
    )
```

time: 175 us -> 62 us (0.35)
  waiting for transfers between devices: 73.1 us -> 0 us
  Pallas kernels: 0 us -> 55.9 us
  local copies, waits for them, and re-layouts: 40.6 us -> 3.26 us
  matrix products: 26.7 us -> 0 us
  between operations: 19.9 us -> 0.02 us
  starting transfers between devices: 9.77 us -> 0 us
    pallas_call x0 -> x1, Pallas kernels: none -> 55.9 us  [local(): pl.pallas_call(functools.partial(kernel, sizes), out_shape=jax.ShapeDtype...]
    ppermute x4 -> x0, waiting for transfers between devices: 46.3 us -> none  [from_behind(): return lax.ppermute(block, axis, route)]
    all_gather x1 -> x0, waiting for transfers between devices: 26.1 us -> none  [local(): all_weights = lax.all_gather(weights, 'batch', axis=0, tiled=True)]
    dot_general x3 -> x0, matrix products: 17.8 us -> none  [the longest x1 6.98 us: attend(): jnp.dot(normed.reshape(-1, width), all_weights[:, :3 * width], preferred_...]
    slice x11 -> x0, local copies, waits for them, and re-layouts: 13.9 us -> none  [the longest x2 5.12 us: attend(): qkv[..., width:2 * width].reshape(num_windows, win_size, HEADS, head_size)]
    ppermute x4 -> x0, starting transfers between devices: 9.77 us -> none  [from_behind(): return lax.ppermute(block, axis, route)]
    transpose x2 -> x0, local copies, waits for them, and re-layouts: 9.02 us -> none  [the longest x1 7.79 us: windows(): field = field.transpose(0, 2, 4, 1, 3, 5, 6)]
    sub x1 -> x0, matrix products: 8.82 us -> none  [attend(): expsc = jnp.exp(scores - largest)]
  transfers between devices with their start and end apart: 5 -> 0, of which waited for: 5 -> 0; matrix products, arithmetic and copies ran while one was open for 3% -> 0% of each run, Pallas kernels for 0% -> 0%
where the time goes in v1:
time: 62 us; the launch traced here: 61.8 us
  Pallas kernels  55.9 us (90%)
  local copies, waits for them, and re-layouts  3.26 us (5%)
  other arithmetic  2.57 us (4%)
    pallas_call x1, Pallas kernels, local(): pl.pallas_call(functools.partial(kernel, sizes), out_shape=jax.ShapeDtype...  55.9 us
    unnamed x1, local copies, waits for them, and re-layouts  2.37 us
    convert_element_type x1, other arithmetic, local(): edge = block[:, :, cols - 1:, :].astype(jnp.float32)  1.71 us

profile of v1, /device:TPU:0, one launch (start us, length us, event | category | flops | bytes accessed | tf_op | source)
XLA Modules:
  0.0 61.8 jit_solution(4505512015104335716)
XLA Ops:
  0.0 0.8 %reshape.5 = s32[2,2,6,2,12]{4,3,0,2,1:T(2,128)S(1)} reshape(s32[2,12,24]{2,0,1:T(2,128)} %param.6) | data formatting | bytes 4608 | tf_op jit(solution)/shard_map/reshape | solution.py:258
  0.8 0.1 eq.15
  0.9 1.7 %slice_convert_fusion.edge_ref = f32[2,12,1,1024]{3,2,1,0:T(1,128)} fusion(bf16[2,12,24,1024]{3,2,1,0:T(8,128)(2,1)} %bitcast.8), kind=kLoop, calls=%fused_computation.1 | loop fusion | flops 24576 | bytes 147456 | tf_op jit(solution)/shard_map/convert_element_type | solution.py:268
  2.6 0.9 %compare_convert_fusion.mask_ref = bf16[2,2,144,144]{3,2,1,0:T(8,128)(2,1)} fusion(s32[2,2,144]{2,1,0:T(2,128)S(1)} %eq.15), kind=kLoop, calls=%fused_computation | loop fusion | flops 165888 | bytes 168192 | tf_op jit(solution)/shard_map/convert_element_type | solution.py:270
  3.5 55.9 %shard_map.46 = bf16[2,12,24,1024]{3,2,1,0:T(8,128)(2,1)} custom-call(s32[2]{0:T(128)} %off_ref.1, bf16[2,12,24,1024]{3,2,1,0:T(8,128)(2,1)} %bitcast.9, bf16[256,4096]{1,0:T(8,128)(2,1)} %w_ref.1, f32[2,12,1,1024]{3,2,1,0:T(1,128)} %slice_convert_fusion.edge_ref, bf16[2,2,144,144]{3,2,1,0:T(8,128)(2,1)} %compare_convert_fusion.mask_ref), custom_call_target="tpu_custom_call" | custom-call | tf_op jit(solution)/shard_map/pallas_call | solution.py:275
  59.4 2.4 %copy.10 = bf16[1,2,12,24,1024]{4,3,2,1,0:T(8,128)(2,1)} copy(bf16[1,2,12,24,1024]{4,3,2,1,0:T(8,128)(2,1)} %bitcast.7) | data formatting | bytes 2359296
  (1 shorter events, 0.0 us)

commit v2 on v1

--- a/solution.py
+++ b/solution.py
@@ -13,6 +13,7 @@
 WLON = 12
 GROUPS = 4
 HALO = WLAT - 1
+OUTS = 2
 MESH = pl.DeviceIdType.MESH
 
 
@@ -25,8 +26,8 @@
 
 def kernel(
     sizes,
-    off_ref, tok_ref, w_ref, edge_ref, mask_ref, out_ref,
-    wqkv, wout, ext, edge_ext, mask, xw, xn, qkv, ow, nat, ret, ymat,
+    off_ref, tok_ref, w_ref, reg_ref, out_ref,
+    wqkv, wout, own, ext, edge, edge_ext, reg_prev, ids, mask, xw, xn, qkv, ow, nat, ret, ymat,
     local_sem, w_send, w_recv, h_send, h_recv, r_send, r_recv, *parts,
 ):
     attn, ret_ext = parts[:GROUPS], parts[GROUPS:]
@@ -36,6 +37,8 @@
     gw = width // GROUPS
     depth = w_ref.shape[0]
     half = depth // 2
+    owid = width // OUTS
+    chunks = GROUPS + OUTS
     chips = nb // 2
     b, lat, lon = lax.axis_index("batch"), lax.axis_index("lat"), lax.axis_index("lon")
     chip, core = b // 2, b % 2
@@ -57,13 +60,15 @@
     ]
 
     def chunk(g):
-        return wqkv.at[g] if g < GROUPS else wout
+        return wqkv.at[g] if g < GROUPS else wout.at[g - GROUPS]
 
     def own_loads(g):
         rows_here = pl.ds(pl.multiple_of(b * depth, depth), depth)
-        if g == GROUPS:
+        if g >= GROUPS:
             return [pltpu.make_async_copy(
-                w_ref.at[:, pl.ds(3 * width, width)], wout.at[rows_here], local_sem.at[3 * g])]
+                w_ref.at[:, pl.ds(3 * width + (g - GROUPS) * owid, owid)],
+                wout.at[g - GROUPS, rows_here],
+                local_sem.at[2 * GROUPS + g])]
         return [
             pltpu.make_async_copy(
                 w_ref.at[:, pl.ds(t * width + g * gw, gw)],
@@ -73,15 +78,15 @@
             for t in range(3)
         ]
 
-    loads = [own_loads(g) for g in range(GROUPS + 1)]
+    loads = [own_loads(g) for g in range(chunks)]
     for group in loads:
         for c in group:
             c.start()
-    tok_load = pltpu.make_async_copy(tok_ref, ext.at[:, 0:rows], local_sem.at[3 * GROUPS + 1])
-    edge_load_sem = local_sem.at[3 * GROUPS + 2]
+    tok_load = pltpu.make_async_copy(tok_ref, own, local_sem.at[3 * GROUPS + OUTS])
+    low_load = pltpu.make_async_copy(
+        tok_ref.at[:, WLAT:rows], ext.at[:, 0:rows - WLAT], local_sem.at[3 * GROUPS + OUTS + 1])
     tok_load.start()
-    mask_load = pltpu.make_async_copy(mask_ref.at[0], mask.at[1], edge_load_sem)
-    mask_load.start()
+    low_load.start()
 
     barrier = pltpu.get_barrier_semaphore()
     for device in greeted:
@@ -110,7 +115,7 @@
 
     xs = {}
     halos = []
-    core_copies = {g: [] for g in range(GROUPS + 1)}
+    core_copies = {g: [] for g in range(chunks)}
     ys = {}
 
     def first(g):
@@ -138,28 +143,67 @@
         for c in core_copies[g]:
             c.wait_recv()
 
-    first(0)
-    halos.append(send(edge_ref, edge_ext.at[:, 0:rows], h_send.at[0], h_recv.at[0], at(dlon=1)))
-    halos.append(send(edge_ref, edge_ext.at[:, rows:2 * rows], h_send.at[1], h_recv.at[1], at(dlat=-1, dlon=1)))
-    halos.append(send(tok_ref.at[:, 0:HALO], ext.at[:, rows:rows + HALO], h_send.at[2], h_recv.at[2], at(dlat=-1)))
-    halos.append(send(mask_ref.at[1], mask.at[0], h_send.at[3], h_recv.at[3], at(dlon=1)))
-    for g in range(1, GROUPS + 1):
+    lat_halo = send(tok_ref.at[:, 0:HALO], ext.at[:, rows - WLAT:rows - WLAT + HALO],
+                    h_send.at[0], h_recv.at[0], at(dlat=-1))
+    reg_halo = send(reg_ref, reg_prev, h_send.at[1], h_recv.at[1], at(dlon=1))
+    for g in range(chunks):
         first(g)
 
     shift = off_ref[0]
-    relay(0)
     tok_load.wait()
-    mask_load.wait()
-    for c in halos:
-        c.wait_recv()
     for l in range(levels):
         for i in range(rows):
-            x = normalise(ext[l, i + shift].astype(jnp.float32))
-            e = normalise(edge_ext[l, i + shift])
-            base = (i // WLAT) * 2 * win + l * WLAT * WLON + (i % WLAT) * WLON
-            xw[base:base + 1, :] = e
-            xw[base + 1:base + WLON, :] = x[0:WLON - 1]
-            xw[base + win:base + win + WLON, :] = x[WLON - 1:2 * WLON - 1]
+            edge[l, i] = own[l, i].astype(jnp.float32)[cols - 1:cols]
+    near_halo = send(edge, edge_ext.at[:, 0:rows], h_send.at[2], h_recv.at[2], at(dlon=1))
+    diag_halo = send(edge, edge_ext.at[:, rows:2 * rows], h_send.at[3], h_recv.at[3], at(dlat=-1, dlon=1))
+    halos = [lat_halo, reg_halo, near_halo, diag_halo]
+
+    def masks(ref, k):
+        for i in range(rows):
+            ids[i * levels:(i + 1) * levels, :] = ref[i].astype(jnp.float32)
+        table = ids[...].astype(jnp.bfloat16)
+        pos = lax.broadcasted_iota(jnp.int32, (levels * rows, win), 1)
+        which = lax.broadcasted_iota(jnp.int32, (levels * rows, win), 0)
+        pos_t = lax.broadcasted_iota(jnp.int32, (win, levels * rows), 0)
+        which_t = lax.broadcasted_iota(jnp.int32, (win, levels * rows), 1)
+        col = (lax.broadcasted_iota(jnp.int32, (cols, win), 0)
+               == k * WLON + lax.broadcasted_iota(jnp.int32, (cols, win), 1) % WLON)
+        col_t = (lax.broadcasted_iota(jnp.int32, (win, cols), 1)
+                 == k * WLON + lax.broadcasted_iota(jnp.int32, (win, cols), 0) % WLON)
+        wide = jnp.dot(table, col.astype(jnp.float32).astype(jnp.bfloat16), preferred_element_type=jnp.float32)
+        tall = lax.dot_general(
+            col_t.astype(jnp.float32).astype(jnp.bfloat16), table, (((1,), (1,)), ((), ())),
+            preferred_element_type=jnp.float32)
+
+        def row_of(p, lw):
+            return (lw * WLAT + p % (WLAT * WLON) // WLON) * levels + p // (WLAT * WLON)
+
+        for lw in range(rows // WLAT):
+            r = jnp.sum(jnp.where(which == row_of(pos, lw), wide, 0.0), 0, keepdims=True)
+            c = jnp.sum(jnp.where(which_t == row_of(pos_t, lw), tall, 0.0), 1, keepdims=True)
+            mask[lw * 2 + 1 - k] = (r == c).astype(jnp.float32)
+
+    def norm(lw):
+        src = own if lw == 0 else ext
+        for l in range(levels):
+            for ii in range(WLAT):
+                x = normalise(src[l, ii + shift].astype(jnp.float32))
+                e = normalise(edge_ext[l, lw * WLAT + ii + shift])
+                base = lw * 2 * win + l * WLAT * WLON + ii * WLON
+                xw[base:base + 1, :] = e
+                xw[base + 1:base + WLON, :] = x[0:WLON - 1]
+                xw[base + win:base + win + WLON, :] = x[WLON - 1:2 * WLON - 1]
+        for w in range(2 * lw, 2 * lw + 2):
+            xn[w * win:(w + 1) * win, :] = xw[w * win:(w + 1) * win, :].astype(jnp.bfloat16)
+
+    masks(reg_ref, 0)
+    relay(0)
+    reg_halo.wait_recv()
+    masks(reg_prev, 1)
+    near_halo.wait_recv()
+    diag_halo.wait_recv()
+    norm(0)
+    relay(1)
     nwin = (rows // WLAT) * (cols // WLON)
     for w in range(nwin):
         xn[w * win:(w + 1) * win, :] = xw[w * win:(w + 1) * win, :].astype(jnp.bfloat16)
@@ -168,16 +212,17 @@
     ones = jnp.ones((win, 128), jnp.bfloat16)
     hs = width // HEADS
 
-    def attention(g):
+    def attention(g, lw):
+        both = slice(lw * 2 * win, (lw + 1) * 2 * win)
         for t in range(3):
             part = jnp.dot(
-                xn[...], wqkv[g, :, t * gw:(t + 1) * gw], preferred_element_type=jnp.float32
+                xn[both, :], wqkv[g, :, t * gw:(t + 1) * gw], preferred_element_type=jnp.float32
             ).astype(jnp.bfloat16)
-            for w in range(nwin):
+            for w in range(2):
                 qkv[w, :, t * gw:(t + 1) * gw] = part[w * win:(w + 1) * win]
 
         def window(w, carry):
-            allowed = mask[w % 2, w // 2].astype(jnp.float32) > 0.5
+            allowed = mask[lw * 2 + w] > 0.5
             for pair in range(gw // 128):
                 q = qkv[w, :, pair * 128:(pair + 1) * 128]
                 k = qkv[w, :, gw + pair * 128:gw + (pair + 1) * 128]
@@ -197,17 +242,18 @@
                 ow[w, :, pair * 128:(pair + 1) * 128] = jnp.where(lane < hs, outs[0], outs[1])
             return carry
 
-        lax.fori_loop(0, nwin, window, 0)
-        gs = slice(g * gw, (g + 1) * gw)
+        lax.fori_loop(0, 2, window, 0)
         for l in range(levels):
-            for i in range(rows):
-                r = l * WLAT * WLON + (i % WLAT) * WLON
-                w = (i // WLAT) * 2
+            for ii in range(WLAT):
+                i = lw * WLAT + ii
+                r = l * WLAT * WLON + ii * WLON
+                w = 0
                 ret[g, l, i] = ow[w, r:r + 1, :].astype(jnp.bfloat16).astype(jnp.float32)
                 nat[l, i, 0:WLON - 1, :] = ow[w, r + 1:r + WLON, :]
                 nat[l, i, WLON - 1:2 * WLON - 1, :] = ow[w + 1, r:r + WLON, :]
                 attn[g][l, HALO + i] = nat[l, i].astype(jnp.bfloat16)
-        back = [
+    def give(g):
+        return [
             send(attn[g].at[:, rows:rows + HALO], attn[g].at[:, 0:HALO],
                  r_send.at[3 * g], r_recv.at[3 * g], at(dlat=1)),
             send(ret.at[g], ret_ext[g].at[:, rows:2 * rows],
@@ -215,7 +261,6 @@
             send(ret.at[g], ret_ext[g].at[:, 0:rows],
                  r_send.at[3 * g + 2], r_recv.at[3 * g + 2], at(dlat=1, dlon=-1)),
         ]
-        return back
 
     nat[:, :, cols - 1:cols, :] = jnp.zeros((levels, rows, 1, gw), jnp.float32)
     row_id = lax.broadcasted_iota(jnp.int32, (cols, gw), 0)
@@ -231,32 +276,37 @@
                 r = (l * rows + i) * cols
                 ymat[r:r + cols, g * gw:(g + 1) * gw] = jnp.where(row_id == cols - 1, e, a)
 
+    finish(0)
+    attention(0, 0)
+    low_load.wait()
+    lat_halo.wait_recv()
+    norm(1)
     for g in range(GROUPS):
-        relay(g + 1)
-        finish(g)
-        backs.append(attention(g))
+        if g > 0:
+            finish(g)
+            attention(g, 0)
+        attention(g, 1)
+        backs.append(give(g))
+        relay(g + 2)
         if g > 0:
             gather(g - 1)
     finish(GROUPS)
+    finish(GROUPS + 1)
     gather(GROUPS - 1)
 
     for l in range(levels):
         for j in range(rows // WLAT):
             r = (l * rows + j * WLAT) * cols
             y = ymat[r:r + WLAT * cols, :].astype(jnp.bfloat16)
-            p = jnp.dot(y, wout[...], preferred_element_type=jnp.float32)
             here = slice(j * WLAT, (j + 1) * WLAT)
-            t = ext[l, here].astype(jnp.float32)
-            out_ref[l, here] = (t + p.reshape(t.shape)).astype(jnp.bfloat16)
+            for n in range(OUTS):
+                side_cols = slice(n * owid, (n + 1) * owid)
+                p = jnp.dot(y, wout[n], preferred_element_type=jnp.float32)
+                t = own[l, here, :, side_cols].astype(jnp.float32)
+                out_ref[l, here, :, side_cols] = (t + p.reshape(t.shape)).astype(jnp.bfloat16)
 
     for c in sent + halos + sum(backs, []):
         c.wait_send()
-
-
-def window_ids(regions):
-    levels, rows, cols = regions.shape
-    field = regions.reshape(levels, rows // WLAT, WLAT, cols // WLON, WLON)
-    return field.transpose(3, 1, 0, 2, 4).reshape(cols // WLON, rows // WLAT, -1)
 
 
 def local(sizes, tokens, weights, regions, offsets):
@@ -265,32 +315,33 @@
     win = WLEV * WLAT * WLON
     nwin = (rows // WLAT) * (cols // WLON)
     gw = width // GROUPS
-    edge = block[:, :, cols - 1:, :].astype(jnp.float32)
-    ids = window_ids(regions)
-    mask = (ids[..., :, None] == ids[..., None, :]).astype(jnp.bfloat16)
-    nw = (GROUPS + 1) * (1 + 4 * (sizes[0] // 2 - 1))
+    nw = (GROUPS + OUTS) * (1 + 4 * (sizes[0] // 2 - 1))
     bf, f32 = jnp.bfloat16, jnp.float32
     dma = pltpu.SemaphoreType.DMA
     anywhere = pl.BlockSpec(memory_space=pl.ANY)
     out = pl.pallas_call(
         functools.partial(kernel, sizes),
         out_shape=jax.ShapeDtypeStruct(block.shape, bf),
-        in_specs=[pl.BlockSpec(memory_space=pltpu.SMEM)] + [anywhere] * 4,
+        in_specs=[pl.BlockSpec(memory_space=pltpu.SMEM), anywhere, anywhere, pl.BlockSpec(memory_space=pltpu.VMEM)],
         out_specs=pl.BlockSpec(memory_space=pltpu.VMEM),
         scratch_shapes=[
             pltpu.VMEM((GROUPS, width, 3 * gw), bf),
-            pltpu.VMEM((width, width), bf),
-            pltpu.VMEM((levels, rows + HALO, cols, width), bf),
+            pltpu.VMEM((OUTS, width, width // OUTS), bf),
+            pltpu.VMEM((levels, rows, cols, width), bf),
+            pltpu.VMEM((levels, rows - WLAT + HALO, cols, width), bf),
+            pltpu.VMEM((levels, rows, 1, width), f32),
             pltpu.VMEM((levels, 2 * rows, 1, width), f32),
-            pltpu.VMEM((2, rows // WLAT, win, win), bf),
+            pltpu.VMEM((rows, levels, cols), jnp.int32),
+            pltpu.VMEM((levels * rows, cols), f32),
+            pltpu.VMEM((nwin, win, win), f32),
             pltpu.VMEM((nwin * win, width), f32),
             pltpu.VMEM((nwin * win, width), bf),
-            pltpu.VMEM((nwin, win, 3 * gw), bf),
-            pltpu.VMEM((nwin, win, gw), f32),
+            pltpu.VMEM((2, win, 3 * gw), bf),
+            pltpu.VMEM((2, win, gw), f32),
             pltpu.VMEM((levels, rows, cols, gw), f32),
             pltpu.VMEM((GROUPS, levels, rows, 1, gw), f32),
             pltpu.VMEM((levels * rows * cols, width), f32),
-            dma((3 * GROUPS + 3,)),
+            dma((3 * GROUPS + OUTS + 2,)),
             dma((nw,)),
             dma((nw,)),
             dma((4,)),
@@ -303,7 +354,7 @@
         compiler_params=pltpu.CompilerParams(
             collective_id=0, has_side_effects=True, vmem_limit_bytes=56 * 1024 * 1024
         ),
-    )(offsets, block, weights, edge, mask)
+    )(offsets, block, weights, regions.transpose(1, 0, 2))
     return out[None]
 
 

time: 62 us -> 58.7 us (0.947)
  other arithmetic: 2.57 us -> 0 us
  local copies, waits for them, and re-layouts: 3.26 us -> 2.37 us
    convert_element_type x2 -> x0, other arithmetic: 2.57 us -> none  [the longest x1 1.71 us: local(): edge = block[:, :, cols - 1:, :].astype(jnp.float32)]
    reshape x2 -> x0, local copies, waits for them, and re-layouts: 0.81 us -> none  [window_ids(): field = regions.reshape(levels, rows // WLAT, WLAT, cols // WLON, WLON)]
where the time goes in v2:
time: 58.7 us; the launch traced here: 58.5 us
  Pallas kernels  56.1 us (96%)
  local copies, waits for them, and re-layouts  2.37 us (4%)
    pallas_call x1, Pallas kernels, local(): pl.pallas_call(functools.partial(kernel, sizes), out_shape=jax.ShapeDtype...  56.1 us
    unnamed x1, local copies, waits for them, and re-layouts  2.37 us

profile of v2, /device:TPU:0, one launch (start us, length us, event | category | flops | bytes accessed | tf_op | source)
XLA Modules:
  0.0 58.5 jit_solution(9344132418519753192)
XLA Ops:
  0.0 56.1 %shard_map.46 = bf16[2,12,24,1024]{3,2,1,0:T(8,128)(2,1)} custom-call(s32[2]{0:T(128)} %off_ref.1, bf16[2,12,24,1024]{3,2,1,0:T(8,128)(2,1)} %bitcast.4, bf16[256,4096]{1,0:T(8,128)(2,1)} %w_ref.1, s32[12,2,24]{2,1,0:T(2,128)} %bitcast.5), custom_call_target="tpu_custom_call" | custom-call | tf_op jit(solution)/shard_map/pallas_call | solution.py:322
  56.1 2.4 %copy.6 = bf16[1,2,12,24,1024]{4,3,2,1,0:T(8,128)(2,1)} copy(bf16[1,2,12,24,1024]{4,3,2,1,0:T(8,128)(2,1)} %bitcast.3) | data formatting | bytes 2359296

commit v3 on v2

--- a/solution.py
+++ b/solution.py
@@ -121,10 +121,12 @@
     def first(g):
         for c in loads[g]:
             c.wait()
+        mine = chunk(g).at[pl.ds(pl.multiple_of(b * depth, depth), depth)]
+        core_copies[g].append(send_w(g, 0, mine, partner))
+
+    def cross(g):
         for k in range(1, chips):
             xs[g, k] = send_w(g, 4 * k - 3, piece(g, b, side), far[k - 1])
-        mine = chunk(g).at[pl.ds(pl.multiple_of(b * depth, depth), depth)]
-        core_copies[g].append(send_w(g, 0, mine, partner))
 
     def origin(k):
         return ((chip + chips - k) % chips) * 2 + core
@@ -132,6 +134,10 @@
     def relay(g):
         for k in range(1, chips):
             xs[g, k].wait_recv()
+        for ahead in ([1, 2] if g == 0 else [g + 2]):
+            if ahead < chunks:
+                cross(ahead)
+        for k in range(1, chips):
             got = piece(g, origin(k), side)
             ys[g, k] = send_w(g, 4 * k - 2, got, across)
             core_copies[g].append(send_w(g, 4 * k - 1, got, partner))
@@ -148,6 +154,8 @@
     reg_halo = send(reg_ref, reg_prev, h_send.at[1], h_recv.at[1], at(dlon=1))
     for g in range(chunks):
         first(g)
+        if g == 0:
+            cross(0)
 
     shift = off_ref[0]
     tok_load.wait()
@@ -242,7 +250,8 @@
                 ow[w, :, pair * 128:(pair + 1) * 128] = jnp.where(lane < hs, outs[0], outs[1])
             return carry
 
-        lax.fori_loop(0, 2, window, 0)
+        for w in range(2):
+            window(w, 0)
         for l in range(levels):
             for ii in range(WLAT):
                 i = lw * WLAT + ii
@@ -285,9 +294,9 @@
         if g > 0:
             finish(g)
             attention(g, 0)
+        relay(g + 2)
         attention(g, 1)
         backs.append(give(g))
-        relay(g + 2)
         if g > 0:
             gather(g - 1)
     finish(GROUPS)

time: 58.7 us -> 56 us (0.954)
  Pallas kernels: 56.1 us -> 53.4 us
    pallas_call x1, Pallas kernels: 56.1 us -> 53.4 us  [local(): pl.pallas_call(functools.partial(kernel, sizes), out_shape=jax.ShapeDtype...]
where the time goes in v3:
time: 56 us; the launch traced here: 55.8 us
  Pallas kernels  53.4 us (95%)
  local copies, waits for them, and re-layouts  2.37 us (4%)
    pallas_call x1, Pallas kernels, local(): pl.pallas_call(functools.partial(kernel, sizes), out_shape=jax.ShapeDtype...  53.4 us
    unnamed x1, local copies, waits for them, and re-layouts  2.37 us

profile of v3, /device:TPU:0, one launch (start us, length us, event | category | flops | bytes accessed | tf_op | source)
XLA Modules:
  0.0 55.8 jit_solution(13807102878227489008)
XLA Ops:
  0.0 53.4 %shard_map.46 = bf16[2,12,24,1024]{3,2,1,0:T(8,128)(2,1)} custom-call(s32[2]{0:T(128)} %off_ref.1, bf16[2,12,24,1024]{3,2,1,0:T(8,128)(2,1)} %bitcast.4, bf16[256,4096]{1,0:T(8,128)(2,1)} %w_ref.1, s32[12,2,24]{2,1,0:T(2,128)} %bitcast.5), custom_call_target="tpu_custom_call" | custom-call | tf_op jit(solution)/shard_map/pallas_call | solution.py:331
  53.4 2.4 %copy.6 = bf16[1,2,12,24,1024]{4,3,2,1,0:T(8,128)(2,1)} copy(bf16[1,2,12,24,1024]{4,3,2,1,0:T(8,128)(2,1)} %bitcast.3) | data formatting | bytes 2359296

commit v4 on v3

--- a/solution.py
+++ b/solution.py
@@ -261,10 +261,14 @@
                 nat[l, i, 0:WLON - 1, :] = ow[w, r + 1:r + WLON, :]
                 nat[l, i, WLON - 1:2 * WLON - 1, :] = ow[w + 1, r:r + WLON, :]
                 attn[g][l, HALO + i] = nat[l, i].astype(jnp.bfloat16)
-    def give(g):
+    def give_rows(g):
         return [
             send(attn[g].at[:, rows:rows + HALO], attn[g].at[:, 0:HALO],
                  r_send.at[3 * g], r_recv.at[3 * g], at(dlat=1)),
+        ]
+
+    def give_edges(g):
+        return [
             send(ret.at[g], ret_ext[g].at[:, rows:2 * rows],
                  r_send.at[3 * g + 1], r_recv.at[3 * g + 1], at(dlon=-1)),
             send(ret.at[g], ret_ext[g].at[:, 0:rows],
@@ -293,10 +297,12 @@
     for g in range(GROUPS):
         if g > 0:
             finish(g)
+        attention(g, 1)
+        back = give_rows(g)
+        relay(g + 2)
+        if g > 0:
             attention(g, 0)
-        relay(g + 2)
-        attention(g, 1)
-        backs.append(give(g))
+        backs.append(back + give_edges(g))
         if g > 0:
             gather(g - 1)
     finish(GROUPS)

time: 56 us -> 55.8 us (level)
  no operation moved by 1% of the time
where the time goes in v4:
time: 55.8 us; the launch traced here: 55.5 us
  Pallas kernels  53.2 us (95%)
  local copies, waits for them, and re-layouts  2.37 us (4%)
    pallas_call x1, Pallas kernels, local(): pl.pallas_call(functools.partial(kernel, sizes), out_shape=jax.ShapeDtype...  53.2 us
    unnamed x1, local copies, waits for them, and re-layouts  2.37 us

profile of v4, /device:TPU:0, one launch (start us, length us, event | category | flops | bytes accessed | tf_op | source)
XLA Modules:
  0.0 55.5 jit_solution(10228342761263606026)
XLA Ops:
  0.0 53.2 %shard_map.46 = bf16[2,12,24,1024]{3,2,1,0:T(8,128)(2,1)} custom-call(s32[2]{0:T(128)} %off_ref.1, bf16[2,12,24,1024]{3,2,1,0:T(8,128)(2,1)} %bitcast.4, bf16[256,4096]{1,0:T(8,128)(2,1)} %w_ref.1, s32[12,2,24]{2,1,0:T(2,128)} %bitcast.5), custom_call_target="tpu_custom_call" | custom-call | tf_op jit(solution)/shard_map/pallas_call | solution.py:337
  53.2 2.4 %copy.6 = bf16[1,2,12,24,1024]{4,3,2,1,0:T(8,128)(2,1)} copy(bf16[1,2,12,24,1024]{4,3,2,1,0:T(8,128)(2,1)} %bitcast.3) | data formatting | bytes 2359296
